TPU v7x, 32 devices: a whole 2x2x4 slice. The times are simulated.
32 devices in a mesh: box: 2 (over core), row: 16 (over z, y, x).
Axes of the slice: x: 2, y: 2, z: 4, core: 2. Of those that a mesh axis runs over, the one named last changes fastest.
Arguments:
- dtn: float32 [4, 6, 384, 2304], P('box', None, 'row'), may hold values from -2 to 8, as said below
- interface_perm: int32 [2, 384], P('box'), may hold values from 0 to 383, each once within a row
Outputs:
- solution_first: float32 [2, 384, 3840], P('box', 'row')
- solution_second: float32 [2, 384, 6144], P('box', 'row')
- merged_map: float32 [2, 8, 384, 6144], P('box', None, 'row')
Inputs may be any that keep to these rules, and one draw needn't show every extreme that they name: `dtn`: each box's map, read as a (2304) x (2304) matrix, is symmetric and positive definite.
All inputs are finite; a program needn't handle non-finite values.
Results may differ from a plain program's by a relative error of at most 0.00012.
Values sent between devices are 32-bit elements; how exact they have to be, the bound alone decides.
A program may use at most 192 MiB of HBM per device.

v0:
```python
import jax
import jax.numpy as jnp
from jax import lax
from jax.sharding import PartitionSpec as P

F = 384


def partner(x, axis, stride):
    return lax.ppermute(x, axis, [(i, i ^ 1 << stride) for i in range(lax.axis_size(axis))])


def product(left, right):
    return jnp.dot(left, right, precision=lax.Precision.HIGHEST)


def block_factor(matrix):
    order = matrix.shape[0]
    block_size = 128
    count_blocks = order // block_size
    panels = []
    inverses = []
    for j in range(count_blocks):
        column = matrix[j * block_size :, j * block_size : (j + 1) * block_size]
        for k in range(j):
            offset = (j - k) * block_size
            column = column - product(panels[k][offset:], panels[k][offset : offset + block_size].T)
        diagonal_block = jnp.linalg.cholesky(column[:block_size])
        inverse = jax.scipy.linalg.solve_triangular(
            diagonal_block, jnp.eye(block_size, dtype=jnp.float32), lower=True
        )
        remainder = product(column[block_size:], inverse.T)
        panels.append(jnp.concatenate([diagonal_block, remainder], axis=0))
        inverses.append(inverse)
    return (panels, inverses, block_size)


def block_solve(factor, rhs):
    panels, inverses, block_size = factor
    count_blocks = len(panels)
    forward = []
    for j in range(count_blocks):
        residue = rhs[j * block_size : (j + 1) * block_size]
        for k in range(j):
            offset = (j - k) * block_size
            residue = residue - product(panels[k][offset : offset + block_size], forward[k])
        forward.append(product(inverses[j], residue))
    backward = [None] * count_blocks
    for j in reversed(range(count_blocks)):
        residue = forward[j]
        for k in range(j + 1, count_blocks):
            offset = (k - j) * block_size
            residue = residue - product(panels[j][offset : offset + block_size].T, backward[k])
        backward[j] = product(inverses[j].T, residue)
    return jnp.concatenate(backward, axis=0)


def slots(matrix, index, width):
    lead = matrix.shape[:-1]
    shaped = matrix.reshape(lead + (matrix.shape[-1] // width, width))
    taken = jnp.take(shaped, index, axis=len(lead))
    return taken.reshape(lead + (index.shape[0] * width,))


def body(dtn, interface_perm):
    first = dtn[0]
    second = dtn[1]
    count = first.shape[1]
    perm = interface_perm[0]
    shared_a, shared_b = (
        lax.all_gather(first[1], "row", axis=0, tiled=True),
        lax.all_gather(second[0], "row", axis=0, tiled=True),
    )
    block_bb = jnp.take(jnp.take(shared_b[:, :F], perm, axis=1), perm, axis=0)
    couple = shared_a[:, F : 2 * F] + block_bb
    outer_a = jnp.concatenate([first[0:1], first[2:6]], axis=0)
    outer_b = second[1:6]
    lift = jnp.concatenate(
        [outer_a[..., F : 2 * F], jnp.take(outer_b[..., :F], perm, axis=-1)], axis=0
    ).reshape(10 * count, F)
    factor = block_factor(couple)
    start = lax.axis_index("row") * count
    select = (
        jnp.arange(F, dtype=jnp.int32)[:, None]
        == start + jnp.arange(count, dtype=jnp.int32)[None, :]
    ).astype(jnp.float32)
    solved = block_solve(factor, jnp.concatenate([lift.T, select], axis=1)).T
    prod_a = product(solved, shared_a)
    placed = jnp.zeros_like(solved).at[:, perm].set(solved)
    prod_b = product(placed, shared_b)
    update = -jnp.concatenate([prod_a[:, :F], prod_a[:, 2 * F :], prod_b[:, F:]], axis=1)
    zero_block = jnp.zeros((5, count, 5 * F), jnp.float32)
    block_a = jnp.concatenate([outer_a[..., :F], outer_a[..., 2 * F :], zero_block], axis=-1)
    block_b = jnp.concatenate([zero_block, outer_b[..., F:]], axis=-1)
    merged = jnp.concatenate([block_a, block_b], axis=0) + update[: 10 * count].reshape(
        10, count, 10 * F
    )
    solution_first = update[10 * count :]
    half = lax.axis_index("box") % 2
    own_s = jnp.stack([2 - half, 7 - half])
    part_s = jnp.stack([1 + half, 6 + half])
    outer_p = jnp.array([0, 1, 3, 4, 5, 6, 8, 9], jnp.int32)
    outer_q = jnp.array([0, 2, 3, 4, 5, 7, 8, 9], jnp.int32)
    own_o = jnp.where(half == 0, outer_p, outer_q)
    part_o = jnp.where(half == 0, outer_q, outer_p)
    own_iface = jnp.take(merged, own_s, axis=0)
    own_outer = jnp.take(merged, own_o, axis=0).reshape(8 * count, 10 * F)
    full_own = lax.all_gather(own_iface, "row", axis=1, tiled=True)
    full_part = partner(full_own, "box", 0)
    own_rows = full_own.reshape(2 * F, 10 * F)
    part_rows = full_part.reshape(2 * F, 10 * F)
    couple_two = slots(own_rows, own_s, F) + slots(part_rows, part_s, F)
    lift_two = slots(own_outer, own_s, F)
    factor_two = block_factor(couple_two)
    select_two = (
        jnp.arange(2 * F, dtype=jnp.int32)[:, None]
        == half * F + start + jnp.arange(count, dtype=jnp.int32)[None, :]
    ).astype(jnp.float32)
    solved_two = block_solve(factor_two, jnp.concatenate([lift_two.T, select_two], axis=1)).T
    own_c = slots(product(solved_two, own_rows), own_o, F)
    part_c = slots(product(solved_two, part_rows), part_o, F)
    base = slots(own_outer, own_o, F) - own_c[: 8 * count]
    cross = -part_c[: 8 * count]
    left_cols = jnp.where(half == 0, base, cross)
    right_cols = jnp.where(half == 0, cross, base)
    merged_two = jnp.concatenate([left_cols, right_cols], axis=1).reshape(1, 8, count, 16 * F)
    sol_own = -own_c[8 * count :]
    sol_part = -part_c[8 * count :]
    sol_left = jnp.where(half == 0, sol_own, sol_part)
    sol_right = jnp.where(half == 0, sol_part, sol_own)
    solution_second = jnp.concatenate([sol_left, sol_right], axis=1)
    return (solution_first[None], solution_second[None], merged_two)


def solution(mesh):
    return jax.shard_map(
        body,
        mesh=mesh,
        in_specs=(P("box", None, "row", None), P("box", None)),
        out_specs=(P("box", "row", None), P("box", "row", None), P("box", None, "row", None)),
        check_vma=False,
    )
```

profile of v0, /device:TPU:1, one launch (start us, length us, event | category | flops | bytes accessed | tf_op | source)
XLA Modules:
  0.0 833.6 jit_solution(4822045302379656813)
XLA Ops:
  38.2 44.4 %all-gather.10.cloned.1.call-done = f32[1,1,384,2304]{3,1,0,2:T(1,128)} async-done(((f32[1,1,24,2304]{3,1,0,2:T(1,128)}), f32[1,1,384,2304]{3,1,0,2:T(1,128)}) %all-gather.10.cloned.1.call-update) | async-done | bytes 3538960 | tf_op jit(solution)/shard_map/all_gather | solution.py:72
  97.4 57.2 %all-gather.8.cloned.1.call-done = f32[1,1,384,2304]{3,1,0,2:T(1,128)} async-done(((f32[1,1,24,2304]{3,1,0,2:T(1,128)}), f32[1,1,384,2304]{3,1,0,2:T(1,128)}) %all-gather.8.cloned.1.call-update) | async-done | bytes 3538960 | tf_op jit(solution)/shard_map/all_gather | solution.py:71
  168.6 13.2 %cholesky.149 = f32[128,128]{1,0:T(8,128)} custom-call(f32[128,128]{1,0:T(8,128)} %fusion.91), custom_call_target="Cholesky" | custom-call | tf_op jit(solution)/shard_map/jit(cholesky)/cholesky | solution.py:28
  185.4 11.3 %custom-call.13 = f32[1,128,128]{1,2,0:T(8,128)} custom-call(f32[1,128,128]{2,1,0:T(8,128)} %fusion.61), custom_call_target="InvertDiagBlocksLowerTriangular" | custom-call | tf_op jit(solution)/shard_map/jit(_solve_triangular)/triangular_solve | solution.py:29
  211.2 13.2 %cholesky.160 = f32[128,128]{1,0:T(8,128)} custom-call(f32[128,128]{1,0:T(8,128)} %fusion.89), custom_call_target="Cholesky" | custom-call | tf_op jit(solution)/shard_map/jit(cholesky)/cholesky | solution.py:28
  228.6 11.3 %custom-call.14 = f32[1,128,128]{1,2,0:T(8,128)} custom-call(f32[1,128,128]{2,1,0:T(8,128)} %fusion.62), custom_call_target="InvertDiagBlocksLowerTriangular" | custom-call | tf_op jit(solution)/shard_map/jit(_solve_triangular)/triangular_solve | solution.py:29
  249.0 13.2 %cholesky.171 = f32[128,128]{1,0:T(8,128)} custom-call(f32[128,128]{1,0:T(8,128)} %fusion.87), custom_call_target="Cholesky" | custom-call | tf_op jit(solution)/shard_map/jit(cholesky)/cholesky | solution.py:28
  265.7 11.3 %custom-call.15 = f32[1,128,128]{1,2,0:T(8,128)} custom-call(f32[1,128,128]{2,1,0:T(8,128)} %fusion.63), custom_call_target="InvertDiagBlocksLowerTriangular" | custom-call | tf_op jit(solution)/shard_map/jit(_solve_triangular)/triangular_solve | solution.py:29
  313.0 143.2 %all-gather.6.cloned.1.call-done = f32[2,384,3840]{2,1,0:T(8,128)} async-done(((f32[2,24,3840]{2,1,0:T(8,128)}), f32[2,384,3840]{2,1,0:T(8,128)}) %all-gather.6.cloned.1.call-update) | async-done | bytes 11796496 | tf_op jit(solution)/shard_map/all_gather | solution.py:108
  490.6 14.9 %reshape.395 = f32[768,10,384]{2,1,0:T(8,128)} reshape(f32[2,384,3840]{2,1,0:T(8,128)} %all-gather.6.cloned.1.call-done) | data formatting | bytes 23592960 | tf_op jit(solution)/shard_map/reshape;reshape | solution.py:60
  505.5 14.5 %copy.156 = f32[768,10,384]{2,0,1:T(8,128)} copy(f32[768,10,384]{2,1,0:T(8,128)} %reshape.395) | data formatting | bytes 23592960 | tf_op jit(solution)/shard_map/reshape;reshape | solution.py:60
  520.0 12.4 %copy.183 = f32[768,3840]{0,1:T(8,128)} copy(f32[768,3840]{1,0:T(8,128)} %bitcast.241) | data formatting | bytes 23592960 | tf_op jit(solution)/shard_map/reshape | solution.py:110
  537.5 14.9 %reshape.396 = f32[768,10,384]{2,1,0:T(8,128)} reshape(f32[2,384,3840]{2,1,0:T(8,128)} %collective-permute-done) | data formatting | bytes 23592960 | tf_op jit(solution)/shard_map/reshape;reshape | solution.py:60
  552.4 14.5 %copy.158 = f32[768,10,384]{2,0,1:T(8,128)} copy(f32[768,10,384]{2,1,0:T(8,128)} %reshape.396) | data formatting | bytes 23592960 | tf_op jit(solution)/shard_map/reshape;reshape | solution.py:60
  579.1 11.7 %cholesky.182 = f32[128,128]{1,0:T(8,128)S(1)} custom-call(f32[128,128]{1,0:T(8,128)S(1)} %fusion.85), custom_call_target="Cholesky" | custom-call | tf_op jit(solution)/shard_map/jit(cholesky)/cholesky | solution.py:28
  613.0 11.9 %cholesky.193 = f32[128,128]{1,0:T(8,128)S(1)} custom-call(f32[128,128]{1,0:T(8,128)S(1)} %fusion.83), custom_call_target="Cholesky" | custom-call | tf_op jit(solution)/shard_map/jit(cholesky)/cholesky | solution.py:28
  640.8 11.7 %cholesky.204 = f32[128,128]{1,0:T(8,128)S(1)} custom-call(f32[128,128]{1,0:T(8,128)S(1)} %fusion.81), custom_call_target="Cholesky" | custom-call | tf_op jit(solution)/shard_map/jit(cholesky)/cholesky | solution.py:28
  669.5 11.7 %cholesky.215 = f32[128,128]{1,0:T(8,128)S(1)} custom-call(f32[128,128]{1,0:T(8,128)S(1)} %fusion.79), custom_call_target="Cholesky" | custom-call | tf_op jit(solution)/shard_map/jit(cholesky)/cholesky | solution.py:28
  695.5 11.9 %cholesky.226 = f32[128,128]{1,0:T(8,128)S(1)} custom-call(f32[128,128]{1,0:T(8,128)S(1)} %fusion.77), custom_call_target="Cholesky" | custom-call | tf_op jit(solution)/shard_map/jit(cholesky)/cholesky | solution.py:28
  722.1 11.7 %cholesky.237 = f32[128,128]{1,0:T(8,128)S(1)} custom-call(f32[128,128]{1,0:T(8,128)S(1)} %fusion.75), custom_call_target="Cholesky" | custom-call | tf_op jit(solution)/shard_map/jit(cholesky)/cholesky | solution.py:28
  735.2 10.0 %custom-call.21 = f32[1,128,128]{1,2,0:T(8,128)S(1)} custom-call(f32[1,128,128]{2,1,0:T(8,128)S(1)} %fusion.69), custom_call_target="InvertDiagBlocksLowerTriangular" | custom-call | tf_op jit(solution)/shard_map/jit(_solve_triangular)/triangular_solve | solution.py:29
  754.2 12.4 %copy.184 = f32[768,3840]{0,1:T(8,128)} copy(f32[768,3840]{1,0:T(8,128)} %bitcast.56) | data formatting | bytes 23592960 | tf_op jit(solution)/shard_map/reshape | solution.py:111
  766.5 14.2 %fusion.8 = f32[216,10,384]{2,0,1:T(8,128)S(1)} fusion(f32[10,384,768]{2,1,0:T(8,128)} %bitcast.240, f32[768,216]{0,1:T(8,128)} %copy-done.9), kind=kOutput, calls=%fused_computation.101 | convolution fusion | flops 7644119040 | bytes 15777792 | tf_op jit(solution)/shard_map/dot_general | solution.py:14
  787.3 13.9 %fusion.10 = f32[216,10,384]{2,0,1:T(8,128)S(1)} fusion(f32[10,384,768]{2,1,0:T(8,128)} %bitcast.239, f32[768,216]{0,1:T(8,128)S(1)} %copy-done.10), kind=kOutput, calls=%fused_computation.103 | convolution fusion | flops 7644119040 | bytes 15777792 | tf_op jit(solution)/shard_map/dot_general | solution.py:14
  (308 shorter events, 307.3 us)
Async XLA Ops:
  7.2 75.4 %all-gather.10.cloned.1.call-start = ((), (), s32[]{:S(2)}) async-start(), calls=%async_computation.2 | async-start | bytes 3760128 | tf_op jit(solution)/shard_map/all_gather | solution.py:72
  8.4 27.4 %copy-start.12 = (f32[1,24,2304]{2,1,0:T(8,128)}, f32[1,24,2304]{2,1,0:T(8,128)S(1)}, u32[]{:S(2)}) copy-start(f32[1,24,2304]{2,1,0:T(8,128)S(1)} %get-tuple-element.19) | copy-start | bytes 663556
  9.4 145.2 %all-gather.8.cloned.1.call-start = ((), (), s32[]{:S(2)}) async-start(), calls=%async_computation.1 | async-start | bytes 3760128 | tf_op jit(solution)/shard_map/all_gather | solution.py:71
  10.3 445.9 %all-gather.6.cloned.1.call-start = ((), (), s32[]{:S(2)}) async-start(), calls=%async_computation | async-start | bytes 12533760 | tf_op jit(solution)/shard_map/all_gather | solution.py:108
  18.5 5.5 copy-start.25
  197.8 9.7 %copy-start.17 = (f32[128,128]{1,0:T(8,128)}, f32[128,128]{1,0:T(8,128)S(1)}, u32[]{:S(2)}) copy-start(f32[128,128]{1,0:T(8,128)S(1)} %fusion.36) | copy-start | bytes 196612
  199.2 6.6 copy-start.8
  200.4 7.1 copy-start.21
  201.8 5.7 copy-start.11
  276.9 8.4 %copy-start.18 = (f32[128,128]{1,0:T(8,128)S(1)}, f32[128,128]{1,0:T(8,128)}, u32[]{:S(2)}) copy-start(f32[128,128]{1,0:T(8,128)} %copy-done.17) | copy-start | bytes 196612
  293.7 9.5 %copy-start = (f32[264,1536]{1,0:T(8,128)S(1)}, f32[264,1536]{1,0:T(8,128)}, u32[]{:S(2)}) copy-start(f32[264,1536]{1,0:T(8,128)} %slice.410) | copy-start | bytes 4866052
  307.4 150.4 %copy-start.30 = (s32[8]{0:T(128)S(1)}, s32[8]{0:T(128)}, u32[]{:S(2)}) copy-start(s32[8]{0:T(128)} %constant.180.clone) | copy-start | bytes 100
  307.4 150.4 %copy-start.31 = (s32[8]{0:T(128)S(1)}, s32[8]{0:T(128)}, u32[]{:S(2)}) copy-start(s32[8]{0:T(128)} %constant.181.clone) | copy-start | bytes 100
  307.4 151.4 %copy-start.29 = (s32[2]{0:T(128)S(1)}, s32[2]{0:T(128)}, u32[]{:S(2)}) copy-start(s32[2]{0:T(128)} %get-tuple-element.14) | copy-start | bytes 28
  456.3 81.2 %collective-permute-start = (f32[2,384,3840]{2,1,0:T(8,128)}, f32[2,384,3840]{2,1,0:T(8,128)}, u32[]{:S(2)}, u32[]{:S(2)}) collective-permute-start(f32[2,384,3840]{2,1,0:T(8,128)} %all-gather.6.cloned.1.call-done), channel_id=1, source_target_pairs={{0,16},{16,0},{1,17},{17,1},{2,18},{18,2},{3,19},{19,3},{4,20},{20... | collective-permute-start | bytes 35389448 | tf_op jit(solution)/shard_map/ppermute | solution.py:10
  458.4 4.9 copy-start.26
  603.4 8.7 %copy-start.16 = (f32[640,128]{0,1:T(8,128)}, f32[640,128]{0,1:T(8,128)S(1)}, u32[]{:S(2)}) copy-start(f32[640,128]{0,1:T(8,128)S(1)} %convolution_subtract_fusion) | copy-start | bytes 983044
  638.0 55.1 %copy-start.24 = (f32[128,216]{0,1:T(8,128)S(1)}, f32[128,216]{0,1:T(8,128)}, u32[]{:S(2)}) copy-start(f32[128,216]{0,1:T(8,128)} %convolution_subtract_fusion.43) | copy-start | bytes 331780
  640.8 53.8 %copy-start.22 = (f32[256,128]{0,1:T(8,128)S(1)}, f32[256,128]{0,1:T(8,128)}, u32[]{:S(2)}) copy-start(f32[256,128]{0,1:T(8,128)} %convolution_subtract_fusion.15) | copy-start | bytes 393220
  669.0 50.1 %copy-start.23 = (f32[128,216]{0,1:T(8,128)S(1)}, f32[128,216]{0,1:T(8,128)}, u32[]{:S(2)}) copy-start(f32[128,216]{0,1:T(8,128)} %convolution_subtract_fusion.40) | copy-start | bytes 331780
  785.0 2.3 copy-start.1
  805.4 2.7 copy-start.3
  810.9 3.4 slice-start
  817.1 3.4 copy-start.4
  (13 other events, 19.7 us)
Sparse Core Ops, SparseCore 0:
  11.3 71.1 all-gather.9
  85.4 69.1 all-gather.7
  313.2 143.0 all-gather.5
where the time goes:
time: 843 us; the launch traced here: 834 us
  other arithmetic  262 us (31%)
  waiting for transfers between devices  245 us (29%)
  local copies, waits for them, and re-layouts  207 us (25%)
  matrix products  102 us (12%)
  between operations  15.8 us (2%)
    all_gather x1, waiting for transfers between devices, body(): full_own = lax.all_gather(own_iface, 'row', axis=1, tiled=True)  143 us
    another operation x27, other arithmetic, block_factor(): diagonal_block = jnp.linalg.cholesky(column[:block_size])  119 us
    another operation x18, other arithmetic, block_factor(): jax.scipy.linalg.solve_triangular(diagonal_block, jnp.eye(block_size, dty...  103 us
    dot_general x83, matrix products, product(): return jnp.dot(left, right, precision=lax.Precision.HIGHEST)  96.5 us
    another operation x4, local copies, waits for them, and re-layouts, slots(): shaped = matrix.reshape(lead + (matrix.shape[-1] // width, width))  58.8 us
    all_gather x1, waiting for transfers between devices, body(): lax.all_gather(first[1], 'row', axis=0, tiled=True)  57.2 us
    all_gather x1, waiting for transfers between devices, body(): lax.all_gather(second[0], 'row', axis=0, tiled=True)  44.4 us
    gather x9, local copies, waits for them, and re-layouts, slots(): taken = jnp.take(shaped, index, axis=len(lead))  30.8 us
  transfers between devices with their start and end apart: 4, of which 3 were waited for; matrix products, arithmetic and copies ran while one was open for 15% of the time, Pallas kernels for 0%

commit v1 on v0

--- a/solution.py
+++ b/solution.py
@@ -63,6 +63,22 @@
 
 
 def body(dtn, interface_perm):
+
+    def spread_meshes_for(arr_in):
+        many = lax.psum(1, "row")
+        blocks_here = []
+        for p in range(many):
+            blocks_here.append((p, (p + 1) % many))
+
+        def make_the_steps_all(odd):
+            if len(odd) == many:
+                return odd
+            return make_the_steps_all([lax.ppermute(odd[0], "row", blocks_here), *odd])
+
+        a_now = make_the_steps_all([arr_in])
+        outcome_arr = jnp.concatenate(a_now, axis=1)
+        return jnp.roll(outcome_arr, shift=(lax.axis_index("row") + 1) * arr_in.shape[1], axis=1)
+
     first = dtn[0]
     second = dtn[1]
     count = first.shape[1]
@@ -105,7 +121,7 @@
     part_o = jnp.where(half == 0, outer_q, outer_p)
     own_iface = jnp.take(merged, own_s, axis=0)
     own_outer = jnp.take(merged, own_o, axis=0).reshape(8 * count, 10 * F)
-    full_own = lax.all_gather(own_iface, "row", axis=1, tiled=True)
+    full_own = spread_meshes_for(own_iface)
     full_part = partner(full_own, "box", 0)
     own_rows = full_own.reshape(2 * F, 10 * F)
     part_rows = full_part.reshape(2 * F, 10 * F)

time: 843 us -> 1030 us (1.22)
  waiting for transfers between devices: 245 us -> 366 us
  local copies, waits for them, and re-layouts: 207 us -> 260 us
  starting transfers between devices: 1.62 us -> 18.6 us
    ppermute x0 -> x15, waiting for transfers between devices: none -> 264 us  [make_the_steps_all(): return make_the_steps_all([lax.ppermute(odd[0], 'row', blocks_here), *odd])]
    all_gather x1 -> x0, waiting for transfers between devices: 143 us -> none  [body(): full_own = lax.all_gather(own_iface, 'row', axis=1, tiled=True)]
    unnamed x72 -> x156, local copies, waits for them, and re-layouts: 18.7 us -> 62 us
    ppermute x1, starting transfers between devices: 1.49 us -> 17.1 us  [partner(): lax.ppermute(x, axis, [(i, i ^ 1 << stride) for i in range(lax.axis_size(...]
    reshape x1 -> x0, local copies, waits for them, and re-layouts: 12.4 us -> none  [body(): own_rows = full_own.reshape(2 * F, 10 * F)]
    dot_general x0 -> x1, local copies, waits for them, and re-layouts: none -> 12.4 us  [product(): return jnp.dot(left, right, precision=lax.Precision.HIGHEST)]
  transfers between devices with their start and end apart: 4 -> 18, of which waited for: 3 -> 17; matrix products, arithmetic and copies ran while one was open for 15% -> 12% of each run, Pallas kernels for 0% -> 0%
where the time goes in v1:
time: 1030 us; the launch traced here: 1020 us
  waiting for transfers between devices  366 us (36%)
  other arithmetic  263 us (26%)
  local copies, waits for them, and re-layouts  260 us (25%)
  matrix products  101 us (10%)
  starting transfers between devices  18.6 us (2%)
  between operations  16 us (2%)
    ppermute x15, waiting for transfers between devices, make_the_steps_all(): return make_the_steps_all([lax.ppermute(odd[0], 'row', blocks_here), *odd])  264 us
    another operation x27, other arithmetic, block_factor(): diagonal_block = jnp.linalg.cholesky(column[:block_size])  119 us
    another operation x18, other arithmetic, block_factor(): jax.scipy.linalg.solve_triangular(diagonal_block, jnp.eye(block_size, dty...  103 us
    dot_general x83, matrix products, product(): return jnp.dot(left, right, precision=lax.Precision.HIGHEST)  95.5 us
    unnamed x156, local copies, waits for them, and re-layouts  62 us
    another operation x4, local copies, waits for them, and re-layouts, slots(): shaped = matrix.reshape(lead + (matrix.shape[-1] // width, width))  59 us
    all_gather x1, waiting for transfers between devices, body(): lax.all_gather(first[1], 'row', axis=0, tiled=True)  57.2 us
    all_gather x1, waiting for transfers between devices, body(): lax.all_gather(second[0], 'row', axis=0, tiled=True)  44.4 us
  transfers between devices with their start and end apart: 18, of which 17 were waited for; matrix products, arithmetic and copies ran while one was open for 12% of the time, Pallas kernels for 0%

profile of v1, /device:TPU:1, one launch (start us, length us, event | category | flops | bytes accessed | tf_op | source)
XLA Modules:
  0.0 1024.0 jit_solution(2195037046829804900)
XLA Ops:
  38.2 44.4 %all-gather.7.cloned.1.call-done = f32[1,1,384,2304]{3,1,0,2:T(1,128)} async-done(((f32[1,1,24,2304]{3,1,0,2:T(1,128)}), f32[1,1,384,2304]{3,1,0,2:T(1,128)}) %all-gather.7.cloned.1.call-update) | async-done | bytes 3538960 | tf_op jit(solution)/shard_map/all_gather | solution.py:88
  97.3 57.2 %all-gather.5.cloned.1.call-done = f32[1,1,384,2304]{3,1,0,2:T(1,128)} async-done(((f32[1,1,24,2304]{3,1,0,2:T(1,128)}), f32[1,1,384,2304]{3,1,0,2:T(1,128)}) %all-gather.5.cloned.1.call-update) | async-done | bytes 3538960 | tf_op jit(solution)/shard_map/all_gather | solution.py:87
  312.5 18.3 %collective-permute-done = f32[2,24,3840]{2,1,0:T(8,128)S(1)} collective-permute-done((f32[2,24,3840]{2,1,0:T(8,128)S(1)}, f32[2,24,3840]{2,1,0:T(8,128)S(1)}, u32[]{:S(2)}, u32[]{:S(2)}) %collective-permute-start) | collective-permute-done | bytes 737312 | tf_op jit(solution)/shard_map/ppermute | solution.py:76
  331.7 18.6 %collective-permute-done.1 = f32[2,24,3840]{2,1,0:T(8,128)S(1)} collective-permute-done((f32[2,24,3840]{2,1,0:T(8,128)S(1)}, f32[2,24,3840]{2,1,0:T(8,128)S(1)}, u32[]{:S(2)}, u32[]{:S(2)}) %collective-permute-start.1) | collective-permute-done | bytes 737312 | tf_op jit(solution)/shard_map/ppermute | solution.py:76
  351.2 17.7 %collective-permute-done.2 = f32[2,24,3840]{2,1,0:T(8,128)S(1)} collective-permute-done((f32[2,24,3840]{2,1,0:T(8,128)S(1)}, f32[2,24,3840]{2,1,0:T(8,128)S(1)}, u32[]{:S(2)}, u32[]{:S(2)}) %collective-permute-start.2) | collective-permute-done | bytes 737312 | tf_op jit(solution)/shard_map/ppermute | solution.py:76
  369.8 16.9 %collective-permute-done.3 = f32[2,24,3840]{2,1,0:T(8,128)S(1)} collective-permute-done((f32[2,24,3840]{2,1,0:T(8,128)S(1)}, f32[2,24,3840]{2,1,0:T(8,128)S(1)}, u32[]{:S(2)}, u32[]{:S(2)}) %collective-permute-start.3) | collective-permute-done | bytes 737312 | tf_op jit(solution)/shard_map/ppermute | solution.py:76
  387.5 16.0 %collective-permute-done.4 = f32[2,24,3840]{2,1,0:T(8,128)S(1)} collective-permute-done((f32[2,24,3840]{2,1,0:T(8,128)S(1)}, f32[2,24,3840]{2,1,0:T(8,128)S(1)}, u32[]{:S(2)}, u32[]{:S(2)}) %collective-permute-start.4) | collective-permute-done | bytes 737312 | tf_op jit(solution)/shard_map/ppermute | solution.py:76
  404.5 15.2 %collective-permute-done.5 = f32[2,24,3840]{2,1,0:T(8,128)S(1)} collective-permute-done((f32[2,24,3840]{2,1,0:T(8,128)S(1)}, f32[2,24,3840]{2,1,0:T(8,128)S(1)}, u32[]{:S(2)}, u32[]{:S(2)}) %collective-permute-start.5) | collective-permute-done | bytes 737312 | tf_op jit(solution)/shard_map/ppermute | solution.py:76
  420.6 14.3 %collective-permute-done.6 = f32[2,24,3840]{2,1,0:T(8,128)S(1)} collective-permute-done((f32[2,24,3840]{2,1,0:T(8,128)S(1)}, f32[2,24,3840]{2,1,0:T(8,128)S(1)}, u32[]{:S(2)}, u32[]{:S(2)}) %collective-permute-start.6) | collective-permute-done | bytes 737312 | tf_op jit(solution)/shard_map/ppermute | solution.py:76
  435.8 14.5 %collective-permute-done.7 = f32[2,24,3840]{2,1,0:T(8,128)S(1)} collective-permute-done((f32[2,24,3840]{2,1,0:T(8,128)S(1)}, f32[2,24,3840]{2,1,0:T(8,128)S(1)}, u32[]{:S(2)}, u32[]{:S(2)}) %collective-permute-start.7) | collective-permute-done | bytes 737312 | tf_op jit(solution)/shard_map/ppermute | solution.py:76
  451.1 15.6 %collective-permute-done.8 = f32[2,24,3840]{2,1,0:T(8,128)S(1)} collective-permute-done((f32[2,24,3840]{2,1,0:T(8,128)S(1)}, f32[2,24,3840]{2,1,0:T(8,128)S(1)}, u32[]{:S(2)}, u32[]{:S(2)}) %collective-permute-start.8) | collective-permute-done | bytes 737312 | tf_op jit(solution)/shard_map/ppermute | solution.py:76
  467.7 16.8 %collective-permute-done.9 = f32[2,24,3840]{2,1,0:T(8,128)S(1)} collective-permute-done((f32[2,24,3840]{2,1,0:T(8,128)S(1)}, f32[2,24,3840]{2,1,0:T(8,128)S(1)}, u32[]{:S(2)}, u32[]{:S(2)}) %collective-permute-start.9) | collective-permute-done | bytes 737312 | tf_op jit(solution)/shard_map/ppermute | solution.py:76
  485.4 18.0 %collective-permute-done.10 = f32[2,24,3840]{2,1,0:T(8,128)S(1)} collective-permute-done((f32[2,24,3840]{2,1,0:T(8,128)S(1)}, f32[2,24,3840]{2,1,0:T(8,128)S(1)}, u32[]{:S(2)}, u32[]{:S(2)}) %collective-permute-start.10) | collective-permute-done | bytes 737312 | tf_op jit(solution)/shard_map/ppermute | solution.py:76
  504.2 19.1 %collective-permute-done.11 = f32[2,24,3840]{2,1,0:T(8,128)S(1)} collective-permute-done((f32[2,24,3840]{2,1,0:T(8,128)S(1)}, f32[2,24,3840]{2,1,0:T(8,128)S(1)}, u32[]{:S(2)}, u32[]{:S(2)}) %collective-permute-start.11) | collective-permute-done | bytes 737312 | tf_op jit(solution)/shard_map/ppermute | solution.py:76
  524.1 20.3 %collective-permute-done.12 = f32[2,24,3840]{2,1,0:T(8,128)S(1)} collective-permute-done((f32[2,24,3840]{2,1,0:T(8,128)S(1)}, f32[2,24,3840]{2,1,0:T(8,128)S(1)}, u32[]{:S(2)}, u32[]{:S(2)}) %collective-permute-start.12) | collective-permute-done | bytes 737312 | tf_op jit(solution)/shard_map/ppermute | solution.py:76
  545.4 21.4 %collective-permute-done.13 = f32[2,24,3840]{2,1,0:T(8,128)} collective-permute-done((f32[2,24,3840]{2,1,0:T(8,128)S(1)}, f32[2,24,3840]{2,1,0:T(8,128)}, u32[]{:S(2)}, u32[]{:S(2)}) %collective-permute-start.13) | collective-permute-done | bytes 737312 | tf_op jit(solution)/shard_map/ppermute | solution.py:76
  567.0 21.2 %collective-permute-done.14 = f32[2,24,3840]{2,1,0:T(8,128)} collective-permute-done((f32[2,24,3840]{2,1,0:T(8,128)}, f32[2,24,3840]{2,1,0:T(8,128)}, u32[]{:S(2)}, u32[]{:S(2)}) %collective-permute-start.14) | collective-permute-done | bytes 737312 | tf_op jit(solution)/shard_map/ppermute | solution.py:76
  633.7 17.1 %collective-permute-start.15 = (f32[2,384,3840]{2,1,0:T(8,128)}, f32[2,384,3840]{2,1,0:T(8,128)}, u32[]{:S(2)}, u32[]{:S(2)}) collective-permute-start(f32[2,384,3840]{2,1,0:T(8,128)} %constant_dynamic-slice_fusion), channel_id=1, source_target_pairs={{0,16},{16,0},{1,17},{17,1},{2,18},{18,2},{3,19},{19,3},{4,20},{20... | collective-permute-start | bytes 35389448 | tf_op jit(solution)/shard_map/ppermute | solution.py:10
  683.6 14.9 %reshape.395 = f32[768,10,384]{2,1,0:T(8,128)} reshape(f32[2,384,3840]{2,1,0:T(8,128)} %constant_dynamic-slice_fusion) | data formatting | bytes 23592960 | tf_op jit(solution)/shard_map/reshape;reshape | solution.py:60
  698.5 14.4 %copy.157 = f32[768,10,384]{2,0,1:T(8,128)} copy(f32[768,10,384]{2,1,0:T(8,128)} %reshape.395) | data formatting | bytes 23592960 | tf_op jit(solution)/shard_map/reshape;reshape | solution.py:60
  730.4 15.2 %reshape.396 = f32[768,10,384]{2,1,0:T(8,128)} reshape(f32[2,384,3840]{2,1,0:T(8,128)} %collective-permute-done.15) | data formatting | bytes 23592960 | tf_op jit(solution)/shard_map/reshape;reshape | solution.py:60
  745.7 14.5 %copy.159 = f32[768,10,384]{2,0,1:T(8,128)} copy(f32[768,10,384]{2,1,0:T(8,128)} %reshape.396) | data formatting | bytes 23592960 | tf_op jit(solution)/shard_map/reshape;reshape | solution.py:60
  957.7 14.0 %fusion.8 = f32[216,10,384]{2,0,1:T(8,128)S(1)} fusion(f32[10,384,768]{2,1,0:T(8,128)} %bitcast.241, f32[768,216]{0,1:T(8,128)} %copy-done.9), kind=kOutput, calls=%fused_computation.101 | convolution fusion | flops 7644119040 | bytes 15777792 | tf_op jit(solution)/shard_map/dot_general | solution.py:14
  978.3 14.0 %fusion.10 = f32[216,10,384]{2,0,1:T(8,128)S(1)} fusion(f32[10,384,768]{2,1,0:T(8,128)} %bitcast.240, f32[768,216]{0,1:T(8,128)S(1)} %copy-done.10), kind=kOutput, calls=%fused_computation.103 | convolution fusion | flops 7644119040 | bytes 15777792 | tf_op jit(solution)/shard_map/dot_general | solution.py:14
  (422 shorter events, 538.4 us)
Async XLA Ops:
  7.2 75.4 %all-gather.7.cloned.1.call-start = ((), (), s32[]{:S(2)}) async-start(), calls=%async_computation.1 | async-start | bytes 3760128 | tf_op jit(solution)/shard_map/all_gather | solution.py:88
  9.4 145.2 %all-gather.5.cloned.1.call-start = ((), (), s32[]{:S(2)}) async-start(), calls=%async_computation | async-start | bytes 3760128 | tf_op jit(solution)/shard_map/all_gather | solution.py:87
  311.3 19.5 %collective-permute-start = (f32[2,24,3840]{2,1,0:T(8,128)S(1)}, f32[2,24,3840]{2,1,0:T(8,128)S(1)}, u32[]{:S(2)}, u32[]{:S(2)}) collective-permute-start(f32[2,24,3840]{2,1,0:T(8,128)S(1)} %broadcast_select_fusion.2), channel_id=1, source_target_pairs={{0,1},{1,2},{2,3},{3,4},{4,5},{5,6},{6,7},{7,8},{8,9},{9,10},{10,1... | collective-permute-start | bytes 2211848 | tf_op jit(solution)/shard_map/ppermute | solution.py:76
  331.7 18.6 %collective-permute-start.1 = (f32[2,24,3840]{2,1,0:T(8,128)S(1)}, f32[2,24,3840]{2,1,0:T(8,128)S(1)}, u32[]{:S(2)}, u32[]{:S(2)}) collective-permute-start(f32[2,24,3840]{2,1,0:T(8,128)S(1)} %collective-permute-done), channel_id=1, source_target_pairs={{0,1},{1,2},{2,3},{3,4},{4,5},{5,6},{6,7},{7,8},{8,9},{9,10},{10,1... | collective-permute-start | bytes 2211848 | tf_op jit(solution)/shard_map/ppermute | solution.py:76
  351.2 17.7 %collective-permute-start.2 = (f32[2,24,3840]{2,1,0:T(8,128)S(1)}, f32[2,24,3840]{2,1,0:T(8,128)S(1)}, u32[]{:S(2)}, u32[]{:S(2)}) collective-permute-start(f32[2,24,3840]{2,1,0:T(8,128)S(1)} %collective-permute-done.1), channel_id=1, source_target_pairs={{0,1},{1,2},{2,3},{3,4},{4,5},{5,6},{6,7},{7,8},{8,9},{9,10},{10,1... | collective-permute-start | bytes 2211848 | tf_op jit(solution)/shard_map/ppermute | solution.py:76
  369.8 16.9 %collective-permute-start.3 = (f32[2,24,3840]{2,1,0:T(8,128)S(1)}, f32[2,24,3840]{2,1,0:T(8,128)S(1)}, u32[]{:S(2)}, u32[]{:S(2)}) collective-permute-start(f32[2,24,3840]{2,1,0:T(8,128)S(1)} %collective-permute-done.2), channel_id=1, source_target_pairs={{0,1},{1,2},{2,3},{3,4},{4,5},{5,6},{6,7},{7,8},{8,9},{9,10},{10,1... | collective-permute-start | bytes 2211848 | tf_op jit(solution)/shard_map/ppermute | solution.py:76
  387.5 16.0 %collective-permute-start.4 = (f32[2,24,3840]{2,1,0:T(8,128)S(1)}, f32[2,24,3840]{2,1,0:T(8,128)S(1)}, u32[]{:S(2)}, u32[]{:S(2)}) collective-permute-start(f32[2,24,3840]{2,1,0:T(8,128)S(1)} %collective-permute-done.3), channel_id=1, source_target_pairs={{0,1},{1,2},{2,3},{3,4},{4,5},{5,6},{6,7},{7,8},{8,9},{9,10},{10,1... | collective-permute-start | bytes 2211848 | tf_op jit(solution)/shard_map/ppermute | solution.py:76
  404.5 15.2 %collective-permute-start.5 = (f32[2,24,3840]{2,1,0:T(8,128)S(1)}, f32[2,24,3840]{2,1,0:T(8,128)S(1)}, u32[]{:S(2)}, u32[]{:S(2)}) collective-permute-start(f32[2,24,3840]{2,1,0:T(8,128)S(1)} %collective-permute-done.4), channel_id=1, source_target_pairs={{0,1},{1,2},{2,3},{3,4},{4,5},{5,6},{6,7},{7,8},{8,9},{9,10},{10,1... | collective-permute-start | bytes 2211848 | tf_op jit(solution)/shard_map/ppermute | solution.py:76
  420.6 14.3 %collective-permute-start.6 = (f32[2,24,3840]{2,1,0:T(8,128)S(1)}, f32[2,24,3840]{2,1,0:T(8,128)S(1)}, u32[]{:S(2)}, u32[]{:S(2)}) collective-permute-start(f32[2,24,3840]{2,1,0:T(8,128)S(1)} %collective-permute-done.5), channel_id=1, source_target_pairs={{0,1},{1,2},{2,3},{3,4},{4,5},{5,6},{6,7},{7,8},{8,9},{9,10},{10,1... | collective-permute-start | bytes 2211848 | tf_op jit(solution)/shard_map/ppermute | solution.py:76
  435.8 14.5 %collective-permute-start.7 = (f32[2,24,3840]{2,1,0:T(8,128)S(1)}, f32[2,24,3840]{2,1,0:T(8,128)S(1)}, u32[]{:S(2)}, u32[]{:S(2)}) collective-permute-start(f32[2,24,3840]{2,1,0:T(8,128)S(1)} %collective-permute-done.6), channel_id=1, source_target_pairs={{0,1},{1,2},{2,3},{3,4},{4,5},{5,6},{6,7},{7,8},{8,9},{9,10},{10,1... | collective-permute-start | bytes 2211848 | tf_op jit(solution)/shard_map/ppermute | solution.py:76
  451.1 15.7 %collective-permute-start.8 = (f32[2,24,3840]{2,1,0:T(8,128)S(1)}, f32[2,24,3840]{2,1,0:T(8,128)S(1)}, u32[]{:S(2)}, u32[]{:S(2)}) collective-permute-start(f32[2,24,3840]{2,1,0:T(8,128)S(1)} %collective-permute-done.7), channel_id=1, source_target_pairs={{0,1},{1,2},{2,3},{3,4},{4,5},{5,6},{6,7},{7,8},{8,9},{9,10},{10,1... | collective-permute-start | bytes 2211848 | tf_op jit(solution)/shard_map/ppermute | solution.py:76
  467.7 16.8 %collective-permute-start.9 = (f32[2,24,3840]{2,1,0:T(8,128)S(1)}, f32[2,24,3840]{2,1,0:T(8,128)S(1)}, u32[]{:S(2)}, u32[]{:S(2)}) collective-permute-start(f32[2,24,3840]{2,1,0:T(8,128)S(1)} %collective-permute-done.8), channel_id=1, source_target_pairs={{0,1},{1,2},{2,3},{3,4},{4,5},{5,6},{6,7},{7,8},{8,9},{9,10},{10,1... | collective-permute-start | bytes 2211848 | tf_op jit(solution)/shard_map/ppermute | solution.py:76
  485.3 18.0 %collective-permute-start.10 = (f32[2,24,3840]{2,1,0:T(8,128)S(1)}, f32[2,24,3840]{2,1,0:T(8,128)S(1)}, u32[]{:S(2)}, u32[]{:S(2)}) collective-permute-start(f32[2,24,3840]{2,1,0:T(8,128)S(1)} %collective-permute-done.9), channel_id=1, source_target_pairs={{0,1},{1,2},{2,3},{3,4},{4,5},{5,6},{6,7},{7,8},{8,9},{9,10},{10,1... | collective-permute-start | bytes 2211848 | tf_op jit(solution)/shard_map/ppermute | solution.py:76
  504.2 19.1 %collective-permute-start.11 = (f32[2,24,3840]{2,1,0:T(8,128)S(1)}, f32[2,24,3840]{2,1,0:T(8,128)S(1)}, u32[]{:S(2)}, u32[]{:S(2)}) collective-permute-start(f32[2,24,3840]{2,1,0:T(8,128)S(1)} %collective-permute-done.10), channel_id=1, source_target_pairs={{0,1},{1,2},{2,3},{3,4},{4,5},{5,6},{6,7},{7,8},{8,9},{9,10},{10,1... | collective-permute-start | bytes 2211848 | tf_op jit(solution)/shard_map/ppermute | solution.py:76
  524.1 20.3 %collective-permute-start.12 = (f32[2,24,3840]{2,1,0:T(8,128)S(1)}, f32[2,24,3840]{2,1,0:T(8,128)S(1)}, u32[]{:S(2)}, u32[]{:S(2)}) collective-permute-start(f32[2,24,3840]{2,1,0:T(8,128)S(1)} %collective-permute-done.11), channel_id=1, source_target_pairs={{0,1},{1,2},{2,3},{3,4},{4,5},{5,6},{6,7},{7,8},{8,9},{9,10},{10,1... | collective-permute-start | bytes 2211848 | tf_op jit(solution)/shard_map/ppermute | solution.py:76
  545.3 21.4 %collective-permute-start.13 = (f32[2,24,3840]{2,1,0:T(8,128)S(1)}, f32[2,24,3840]{2,1,0:T(8,128)}, u32[]{:S(2)}, u32[]{:S(2)}) collective-permute-start(f32[2,24,3840]{2,1,0:T(8,128)S(1)} %collective-permute-done.12), channel_id=1, source_target_pairs={{0,1},{1,2},{2,3},{3,4},{4,5},{5,6},{6,7},{7,8},{8,9},{9,10},{10,1... | collective-permute-start | bytes 2211848 | tf_op jit(solution)/shard_map/ppermute | solution.py:76
  566.8 21.4 %collective-permute-start.14 = (f32[2,24,3840]{2,1,0:T(8,128)}, f32[2,24,3840]{2,1,0:T(8,128)}, u32[]{:S(2)}, u32[]{:S(2)}) collective-permute-start(f32[2,24,3840]{2,1,0:T(8,128)} %collective-permute-done.13), channel_id=1, source_target_pairs={{0,1},{1,2},{2,3},{3,4},{4,5},{5,6},{6,7},{7,8},{8,9},{9,10},{10,1... | collective-permute-start | bytes 2211848 | tf_op jit(solution)/shard_map/ppermute | solution.py:76
  567.0 29.4 %copy-start.30 = (f32[2,24,3840]{2,1,0:T(8,128)S(1)}, f32[2,24,3840]{2,1,0:T(8,128)}, u32[]{:S(2)}) copy-start(f32[2,24,3840]{2,1,0:T(8,128)} %copy-done.29) | copy-start | bytes 2211844
  633.7 96.7 %collective-permute-start.15 = (f32[2,384,3840]{2,1,0:T(8,128)}, f32[2,384,3840]{2,1,0:T(8,128)}, u32[]{:S(2)}, u32[]{:S(2)}) collective-permute-start(f32[2,384,3840]{2,1,0:T(8,128)} %constant_dynamic-slice_fusion), channel_id=1, source_target_pairs={{0,16},{16,0},{1,17},{17,1},{2,18},{18,2},{3,19},{19,3},{4,20},{20... | collective-permute-start | bytes 35389448 | tf_op jit(solution)/shard_map/ppermute | solution.py:10
  805.1 53.8 %copy-start.51 = (f32[128,216]{0,1:T(8,128)S(1)}, f32[128,216]{0,1:T(8,128)}, u32[]{:S(2)}) copy-start(f32[128,216]{0,1:T(8,128)} %convolution_subtract_fusion.45) | copy-start | bytes 331780
  805.1 54.5 %copy-start.47 = (f32[384,128]{0,1:T(8,128)S(1)}, f32[384,128]{0,1:T(8,128)}, u32[]{:S(2)}) copy-start(f32[384,128]{0,1:T(8,128)} %convolution_subtract_fusion.5) | copy-start | bytes 589828
  805.2 79.0 %copy-start.50 = (f32[128,216]{0,1:T(8,128)S(1)}, f32[128,216]{0,1:T(8,128)}, u32[]{:S(2)}) copy-start(f32[128,216]{0,1:T(8,128)} %convolution_subtract_fusion.43) | copy-start | bytes 331780
  831.0 54.6 %copy-start.48 = (f32[256,128]{0,1:T(8,128)S(1)}, f32[256,128]{0,1:T(8,128)}, u32[]{:S(2)}) copy-start(f32[256,128]{0,1:T(8,128)} %convolution_subtract_fusion.15) | copy-start | bytes 393220
  857.6 52.8 %copy-start.49 = (f32[128,216]{0,1:T(8,128)S(1)}, f32[128,216]{0,1:T(8,128)}, u32[]{:S(2)}) copy-start(f32[128,216]{0,1:T(8,128)} %convolution_subtract_fusion.40) | copy-start | bytes 331780
  (53 other events, 315.8 us)
Sparse Core Ops, SparseCore 0:
  11.3 71.1 all-gather.6
  85.3 69.1 all-gather.4
